TPU v7x, 256 devices: a whole 4x4x8 slice. The times are simulated.
256 devices in a mesh: region: 64 (over x, z, core), level: 4 (over y).
Axes of the slice: x: 4, y: 4, z: 8, core: 2. Of those that a mesh axis runs over, the one named last changes fastest.
Arguments:
- ensemble: bfloat16 [4, 256, 262144], P('level', None, 'region'), may hold values from -6 to 6
- obs_anomaly: bfloat16 [4, 65536, 256], P('level', 'region'), may hold values from -6 to 6
- innovation: bfloat16 [4, 65536], P('level', 'region'), may hold values from -18 to 18
- obs_precision: bfloat16 [4, 65536], P('level', 'region'), may hold values from 0.019897461 to 0.29882812
- owner_region: int32 [4, 65536, 1], P('level', 'region'), may hold values from 0 to 63; in each aligned block of 1024 rows (0 to 1023, 1024 to 2047, ..., all dimensions but the last counted through in order) at most 24 rows name the same one
- neighbours: int32 [64, 3], replicated, may hold values from 0 to 63, all different within a row
Outputs:
- analysis: bfloat16 [4, 256, 262144], P('level', None, 'region')
Inputs may be any that keep to these rules, and one draw needn't show every extreme that they name: `owner_region`: among the 1024 observations of one device (aligned blocks), no region is named more than 24 times, a bound that some block reaches. `neighbours`: each row lists 3 different regions; every region is listed by some row.
All inputs are finite; a program needn't handle non-finite values.
Results may differ from a plain program's by a relative error of at most 0.0059.
Values may be sent and summed in bfloat16 or wider, within the bound.
No kernel may reach another device: no remote copies, remote signals or barrier semaphores. Data moves between devices by JAX's collectives and lax.ppermute only.
A program may use at most 64 MiB of HBM per device.

v0:
```python
import math
import jax
import jax.numpy as jnp
from jax import lax
from jax.sharding import PartitionSpec as P

NSTEPS = 4
TAPER = 0.6


def cut_along(value, dim, count):
    before, after = (value.shape[:dim], value.shape[dim + 1 :])
    return jnp.moveaxis(value.reshape(*before, count, -1, *after), dim, 0)


def sum_at_owner(value, axis, dim):
    count = lax.axis_size(axis)
    pieces = lax.all_to_all(cut_along(value, dim, count), axis, 0, 0, tiled=True)
    return jnp.sum(pieces, axis=0)


def neighbour_weights(neighbours):
    region_ids = jnp.arange(neighbours.shape[0], dtype=jnp.int32)
    weights = (region_ids[:, None] == region_ids[None, :]).astype(jnp.float32)
    for listed in range(neighbours.shape[1]):
        hit = (neighbours[:, listed][:, None] == region_ids[None, :]).astype(jnp.float32)
        weights = weights + TAPER ** (listed + 1) * hit
    return weights


def inverse_root(matrix):
    order_size = matrix.shape[0]
    identity = jnp.eye(order_size, dtype=jnp.float32)
    norm_scale = 0.5 * jnp.sqrt(jnp.sum(matrix * matrix))
    root_iter = matrix / norm_scale
    inverse_iter = identity
    for newton_step in range(NSTEPS):
        correction = 1.5 * identity - 0.5 * jnp.dot(
            inverse_iter, root_iter, precision=lax.Precision.HIGHEST
        )
        root_iter = jnp.dot(root_iter, correction, precision=lax.Precision.HIGHEST)
        inverse_iter = jnp.dot(correction, inverse_iter, precision=lax.Precision.HIGHEST)
    return inverse_iter / jnp.sqrt(norm_scale)


def analysis_weights(covariance, innovation_sum):
    order_size = covariance.shape[0]
    identity = jnp.eye(order_size, dtype=jnp.float32)
    precision_matrix = covariance + (order_size - 1.0) * identity
    root = inverse_root(precision_matrix)
    inner = jnp.dot(root, innovation_sum, precision=lax.Precision.HIGHEST)
    mean_shift = jnp.dot(root, inner, precision=lax.Precision.HIGHEST)
    return (math.sqrt(order_size - 1.0) * root + mean_shift[:, None]).astype(jnp.bfloat16)


def update_columns(column_block, transform):
    average = jnp.mean(column_block.astype(jnp.float32), axis=0)
    anomaly = (column_block.astype(jnp.float32) - average[None, :]).astype(jnp.bfloat16)
    combined = lax.dot_general(
        transform, anomaly, (((0,), (0,)), ((), ())), preferred_element_type=jnp.float32
    )
    return (combined + average[None, :]).astype(jnp.bfloat16)


def level_factor(distance, levels):
    factor = jnp.zeros(distance.shape, jnp.float32)
    for apart in range(levels):
        factor = factor + 0.5**apart * (distance == apart).astype(jnp.float32)
    return factor


def body(ensemble, obs_anomaly, innovation, obs_precision, owner_region, neighbours):
    regions = lax.axis_size("region")
    levels = lax.axis_size("level")
    my_level = lax.axis_index("level")
    members = obs_anomaly.shape[2]
    local_obs = obs_anomaly.shape[1]
    capacity = 3 * local_obs // (2 * regions)
    slot_count = (neighbours.shape[1] + 1) * capacity
    region_weight = neighbour_weights(neighbours)
    owner_ids = owner_region[0, :, 0]
    region_ids = jnp.arange(regions, dtype=jnp.int32)
    owner_table = (owner_ids[:, None] == region_ids[None, :]).astype(jnp.float32)
    dest_weight = jnp.dot(owner_table, region_weight.T, precision=lax.Precision.HIGHEST)
    live = dest_weight > 0
    position = jnp.cumsum(live.astype(jnp.int32), axis=0) - 1
    gain = (dest_weight * obs_precision[0].astype(jnp.float32)[:, None]).astype(jnp.bfloat16)
    slot_ids = jnp.arange(slot_count, dtype=jnp.int32)
    placement = jnp.logical_and(
        live.T[:, None, :], position.T[:, None, :] == slot_ids[None, :, None]
    )
    place_float = placement.astype(jnp.float32)
    send_rows = jnp.einsum(
        "rso,om->rsm",
        placement.astype(jnp.bfloat16),
        obs_anomaly[0],
        preferred_element_type=jnp.float32,
    ).astype(jnp.bfloat16)
    send_gain = jnp.einsum(
        "rso,or->rs", place_float, gain.astype(jnp.float32), precision=lax.Precision.HIGHEST
    ).astype(jnp.bfloat16)
    send_innov = jnp.einsum(
        "rso,o->rs", place_float, innovation[0].astype(jnp.float32), precision=lax.Precision.HIGHEST
    ).astype(jnp.bfloat16)
    received = (
        lax.all_to_all(send_rows, "region", split_axis=0, concat_axis=0, tiled=True),
        lax.all_to_all(send_gain, "region", split_axis=0, concat_axis=0, tiled=True),
        lax.all_to_all(send_innov, "region", split_axis=0, concat_axis=0, tiled=True),
    )
    routed_rows = received[0].reshape(-1, members)
    routed_gain = received[1].reshape(-1)
    routed_innov = received[2].reshape(-1)
    weighted = (routed_gain.astype(jnp.float32)[:, None] * routed_rows.astype(jnp.float32)).astype(
        jnp.bfloat16
    )
    own_cov = jnp.dot(weighted.T, routed_rows, preferred_element_type=jnp.float32)
    own_sum = jnp.dot(routed_innov, weighted, preferred_element_type=jnp.float32)
    stacked = jnp.tile(own_cov, (levels, 1))
    target_level = jnp.arange(members * lax.axis_size("level"), dtype=jnp.int32) // members
    factor = level_factor(jnp.abs(target_level - my_level), levels)
    covariance = sum_at_owner(factor[:, None] * stacked, "level", 0)
    level_ids = jnp.arange(levels, dtype=jnp.int32)
    sum_terms = level_factor(jnp.abs(level_ids - my_level), levels)[:, None] * own_sum[None, :]
    all_sums = lax.psum(sum_terms, "level")
    innovation_sum = lax.dynamic_index_in_dim(all_sums, my_level, 0, keepdims=False)
    transform = analysis_weights(covariance, innovation_sum)
    return update_columns(ensemble[0], transform)[None]


def solution(mesh):
    return jax.shard_map(
        body,
        mesh=mesh,
        in_specs=(
            P("level", None, "region"),
            P("level", "region", None),
            P("level", "region"),
            P("level", "region"),
            P("level", "region", None),
            P(),
        ),
        out_specs=P("level", None, "region"),
        check_vma=False,
    )
```

profile of v0, /device:TPU:2, one launch (start us, length us, event | category | flops | bytes accessed | tf_op | source)
XLA Modules:
  0.0 175.8 jit_solution(10290218327440279134)
XLA Ops:
  0.0 0.0 copy-start
  0.0 0.8 slice_bitcast_fusion.2
  0.8 0.7 convert_element_type.111
  1.5 1.2 fusion.32
  2.9 18.0 %reduce-window.6 = s32[64,8,128]{2,1,0:T(8,128)S(1)} reduce-window(s32[64,8,128]{2,1,0:T(8,128)S(1)} %bitcast.82, s32[]{:T(128)} %constant.70.clone.1), window={size=1x1x128 pad=0_0x0_0x127_0}, to_apply=%region_0.0 | reduce-window | flops 8323072 | bytes 524292 | tf_op jit(solution)/shard_map/reduce-window
  20.9 0.1 slice.20
  21.0 0.1 copy.15
  21.2 0.1 copy.16
  21.3 0.1 add_add_fusion
  21.5 4.8 %fusion.5 = f32[64,1,96]{2,1,0:T(1,128)S(1)} fusion(s32[64,1024]{1,0:T(8,128)S(1)} %bitcast.84, pred[64,1024]{1,0:T(8,128)(4,1)S(1)} %get-tuple-element.6, bf16[1024,64,1]{0,1,2:T(8,128)(2,1)S(1)} %fusion.37), kind=kOutput, calls=%fused_computation.4 | convolution fusion | flops 25165824 | bytes 483328 | tf_op jit(solution)/shard_map/rso,or->rs/dot_general | solution.py:99
  26.2 0.6 copy.17
  26.9 12.0 %all-to-all-start = ((bf16[64,1,96]{2,1,0:T(2,128)(2,1)}), bf16[64,1,96]{2,1,0:T(2,128)(2,1)S(1)}, u32[]{:S(2)}, u32[]{:S(2)}) async-start(bf16[64,1,96]{2,1,0:T(2,128)(2,1)} %copy.17), calls=%async_computation | async-start | bytes 65536 | tf_op jit(solution)/shard_map/all_to_all | solution.py:107
  38.9 0.0 copy-done
  38.9 6.9 %fusion.21 = bf16[64,96,256]{2,1,0:T(8,128)(2,1)} fusion(s32[64,1024]{1,0:T(8,128)S(1)} %bitcast.85, pred[64,1024]{1,0:T(8,128)(4,1)S(1)} %get-tuple-element.6, bf16[1,1024,256]{2,1,0:T(8,128)(2,1)S(1)} %copy-done), kind=kOutput, calls=%fused_computation.23 | convolution fusion | flops 3235381248 | bytes 3997696 | tf_op jit(solution)/shard_map/rso,om->rsm/dot_general | solution.py:93
  45.8 1.7 all-to-all-done
  47.5 9.0 %all-to-all-start.1 = ((bf16[64,96,256]{2,1,0:T(8,128)(2,1)}), bf16[64,96,256]{2,1,0:T(8,128)(2,1)}, u32[]{:S(2)}, u32[]{:S(2)}) async-start(bf16[64,96,256]{2,1,0:T(8,128)(2,1)} %fusion.21), calls=%async_computation.1 | async-start | bytes 6291456 | tf_op jit(solution)/shard_map/all_to_all | solution.py:106
  56.5 0.0 copy-done.2
  56.5 0.0 copy-start.1
  56.5 4.7 %fusion.1 = f32[1,64,96]{2,0,1:T(1,128)S(1)} fusion(s32[64,1024]{1,0:T(8,128)S(1)} %bitcast.86, pred[64,1024]{1,0:T(8,128)(4,1)S(1)} %get-tuple-element.6, bf16[1,1024]{1,0:T(2,128)(2,1)S(1)} %copy-done.2), kind=kOutput, calls=%fused_computation.2 | convolution fusion | flops 25165824 | bytes 354304 | tf_op jit(solution)/shard_map/rso,o->rs/dot_general | solution.py:102
  61.2 0.6 copy.18
  61.8 0.0 copy-done.1
  61.8 0.3 convert_reduce_fusion
  62.2 66.1 %all-to-all-done.1 = bf16[64,96,256]{2,1,0:T(8,128)(2,1)} async-done(((bf16[64,96,256]{2,1,0:T(8,128)(2,1)}), bf16[64,96,256]{2,1,0:T(8,128)(2,1)}, u32[]{:S(2)}, u32[]{:S(2)}) %all-to-all-start.1) | async-done | bytes 3145760 | tf_op jit(solution)/shard_map/all_to_all | solution.py:106
  128.3 7.3 %all-to-all-start.3 = ((bf16[64,1,96]{2,1,0:T(2,128)(2,1)}), bf16[64,1,96]{2,1,0:T(2,128)(2,1)S(1)}, u32[]{:S(2)}, u32[]{:S(2)}) async-start(bf16[64,1,96]{2,1,0:T(2,128)(2,1)} %copy.18), calls=%async_computation.3 | async-start | bytes 65536 | tf_op jit(solution)/shard_map/all_to_all | solution.py:108
  135.6 4.8 %fusion.30 = f32[256,256]{1,0:T(8,128)S(1)} fusion(bf16[64,96,256]{2,1,0:T(8,128)(2,1)} %all-to-all-done.1, f32[64,96]{1,0:T(8,128)S(1)} %bitcast.89), kind=kOutput, calls=%fused_computation.34 | convolution fusion | flops 810024960 | bytes 3432448 | tf_op jit(solution)/shard_map/dot_general | solution.py:116
  140.4 1.2 broadcast_multiply_fusion
  141.6 2.7 %all-to-all-done.3 = bf16[64,1,96]{2,1,0:T(2,128)(2,1)S(1)} async-done(((bf16[64,1,96]{2,1,0:T(2,128)(2,1)}), bf16[64,1,96]{2,1,0:T(2,128)(2,1)S(1)}, u32[]{:S(2)}, u32[]{:S(2)}) %all-to-all-start.3) | async-done | bytes 12320 | tf_op jit(solution)/shard_map/all_to_all | solution.py:108
  144.2 4.5 %all-to-all-start.2 = ((f32[4,256,256]{2,1,0:T(8,128)}), f32[4,256,256]{2,1,0:T(8,128)}, u32[]{:S(2)}, u32[]{:S(2)}) async-start(f32[4,256,256]{2,1,0:T(8,128)} %broadcast_multiply_fusion), calls=%async_computation.2 | async-start | bytes 2097152 | tf_op jit(solution)/shard_map/all_to_all | solution.py:18
  148.7 2.6 %fusion.15 = f32[1,256,1]{1,0,2:T(1,128)S(1)} fusion(bf16[64,96,256]{2,1,0:T(8,128)(2,1)} %all-to-all-done.1, f32[64,96]{1,0:T(8,128)S(1)} %bitcast.90, bf16[64,1,96]{2,1,0:T(2,128)(2,1)S(1)} %all-to-all-done.3), kind=kOutput, calls=%fused_computation.17 | convolution fusion | flops 7864320 | bytes 3183616 | tf_op jit(solution)/shard_map/dot_general | solution.py:117
  151.3 0.1 broadcast_multiply_fusion.2
  151.4 14.7 %psum.7 = f32[4,256]{1,0:T(4,128)S(1)} all-reduce(f32[4,256]{1,0:T(4,128)S(1)} %broadcast_multiply_fusion.2), channel_id=1, replica_groups=mesh['region'=64,'level'=4] {'level'}, use_global_device_ids=true, to_apply=%region_4.5 | all-reduce | flops 1024 | bytes 8192 | tf_op jit(solution)/shard_map/psum | solution.py:124
  166.1 0.0 all-to-all-done.2
  166.1 1.3 reduce_sum.27
  167.4 0.7 multiply_reduce_fusion
  168.8 0.3 fusion.29
  169.2 0.4 fusion.40
  169.6 0.3 fusion.34
  169.9 0.4 fusion.28
  170.2 0.4 fusion.78
  170.6 0.4 fusion.77
  171.0 0.4 fusion.27
  171.4 0.4 fusion.79
  171.8 0.4 fusion.80
  172.2 0.4 fusion.26
  172.6 0.4 convolution_divide_fusion
  173.0 0.3 convolution_bitcast_fusion
  173.2 0.3 fusion.81
  173.6 2.2 %fusion.14 = bf16[1,256,4096]{2,1,0:T(8,128)(2,1)} fusion(bf16[1,256,4096]{2,1,0:T(8,128)(2,1)S(1)} %copy-done.1, f32[4096]{0:T(1024)S(1)} %broadcast_multiply_fusion.1, f32[256,256]{1,0:T(8,128)S(1)} %convolution_divide_fusion, f32[256]{0:T(256)S(1)} %bitcast.93), kind=kOutput, calls=%fused_computation.16 | convolution fusion | flops 542310400 | bytes 4473856 | tf_op jit(solution)/shard_map/dot_general | solution.py:59
  (13 shorter events, 0.3 us)
Async XLA Ops:
  0.0 38.9 %copy-start = (bf16[1,1024,256]{2,1,0:T(8,128)(2,1)S(1)}, bf16[1,1024,256]{2,1,0:T(8,128)(2,1)}, u32[]{:S(2)}) copy-start(bf16[1,1024,256]{2,1,0:T(8,128)(2,1)} %param.7) | copy-start | bytes 1572868
  26.9 20.6 %all-to-all-start = ((bf16[64,1,96]{2,1,0:T(2,128)(2,1)}), bf16[64,1,96]{2,1,0:T(2,128)(2,1)S(1)}, u32[]{:S(2)}, u32[]{:S(2)}) async-start(bf16[64,1,96]{2,1,0:T(2,128)(2,1)} %copy.17), calls=%async_computation | async-start | bytes 65536 | tf_op jit(solution)/shard_map/all_to_all | solution.py:107
  45.8 10.7 %copy-start.2 = (bf16[1,1024]{1,0:T(2,128)(2,1)S(1)}, bf16[1,1024]{1,0:T(2,128)(2,1)}, u32[]{:S(2)}) copy-start(bf16[1,1024]{1,0:T(2,128)(2,1)} %param.8) | copy-start | bytes 6148
  47.5 80.9 %all-to-all-start.1 = ((bf16[64,96,256]{2,1,0:T(8,128)(2,1)}), bf16[64,96,256]{2,1,0:T(8,128)(2,1)}, u32[]{:S(2)}, u32[]{:S(2)}) async-start(bf16[64,96,256]{2,1,0:T(8,128)(2,1)} %fusion.21), calls=%async_computation.1 | async-start | bytes 6291456 | tf_op jit(solution)/shard_map/all_to_all | solution.py:106
  56.5 5.3 %copy-start.1 = (bf16[1,256,4096]{2,1,0:T(8,128)(2,1)S(1)}, bf16[1,256,4096]{2,1,0:T(8,128)(2,1)}, u32[]{:S(2)}) copy-start(bf16[1,256,4096]{2,1,0:T(8,128)(2,1)} %param.6) | copy-start | bytes 6291460
  128.3 15.9 %all-to-all-start.3 = ((bf16[64,1,96]{2,1,0:T(2,128)(2,1)}), bf16[64,1,96]{2,1,0:T(2,128)(2,1)S(1)}, u32[]{:S(2)}, u32[]{:S(2)}) async-start(bf16[64,1,96]{2,1,0:T(2,128)(2,1)} %copy.18), calls=%async_computation.3 | async-start | bytes 65536 | tf_op jit(solution)/shard_map/all_to_all | solution.py:108
  144.2 21.9 %all-to-all-start.2 = ((f32[4,256,256]{2,1,0:T(8,128)}), f32[4,256,256]{2,1,0:T(8,128)}, u32[]{:S(2)}, u32[]{:S(2)}) async-start(f32[4,256,256]{2,1,0:T(8,128)} %broadcast_multiply_fusion), calls=%async_computation.2 | async-start | bytes 2097152 | tf_op jit(solution)/shard_map/all_to_all | solution.py:18
where the time goes:
time: 176 us
  waiting for transfers between devices  70.4 us (40%)
  starting transfers between devices  32.7 us (19%)
  matrix products  31.8 us (18%)
  other arithmetic  22.6 us (13%)
  blocking collectives  14.7 us (8%)
  local copies, waits for them, and re-layouts  2.54 us (1%)
    all_to_all x1, waiting for transfers between devices, body(): lax.all_to_all(send_rows, 'region', split_axis=0, concat_axis=0, tiled=True)  66.1 us
    another operation x2, other arithmetic  18 us
    psum x1, blocking collectives, body(): all_sums = lax.psum(sum_terms, 'level')  14.7 us
    all_to_all x1, starting transfers between devices, body(): lax.all_to_all(send_gain, 'region', split_axis=0, concat_axis=0, tiled=True)  12 us
    all_to_all x1, starting transfers between devices, body(): lax.all_to_all(send_rows, 'region', split_axis=0, concat_axis=0, tiled=True)  8.98 us
    all_to_all x1, starting transfers between devices, body(): lax.all_to_all(send_innov, 'region', split_axis=0, concat_axis=0, tiled=T...  7.27 us
    dot_general x1, matrix products, body(): jnp.einsum('rso,om->rsm', placement.astype(jnp.bfloat16), obs_anomaly[0],...  6.88 us
    dot_general x1, matrix products, body(): jnp.dot(weighted.T, routed_rows, preferred_element_type=jnp.float32)  4.79 us
  transfers between devices with their start and end apart: 4, of which 3 were waited for; matrix products, arithmetic and copies ran while one was open for 12% of the time, Pallas kernels for 0%

commit v1 on v0

--- a/solution.py
+++ b/solution.py
@@ -121,7 +121,10 @@
     covariance = sum_at_owner(factor[:, None] * stacked, "level", 0)
     level_ids = jnp.arange(levels, dtype=jnp.int32)
     sum_terms = level_factor(jnp.abs(level_ids - my_level), levels)[:, None] * own_sum[None, :]
-    all_sums = lax.psum(sum_terms, "level")
+    size, all_sums = (lax.axis_size("level"), sum_terms)
+    for reach in [1 << k for k in range(size.bit_length() - 1)]:
+        swap = [(i, i ^ reach) for i in range(size)]
+        all_sums = all_sums + lax.ppermute(all_sums, "level", swap)
     innovation_sum = lax.dynamic_index_in_dim(all_sums, my_level, 0, keepdims=False)
     transform = analysis_weights(covariance, innovation_sum)
     return update_columns(ensemble[0], transform)[None]

time: 176 us -> 176 us (level)
  blocking collectives: 14.7 us -> 0 us
  waiting for transfers between devices: 70.4 us -> 79.5 us
  starting transfers between devices: 32.7 us -> 37.5 us
    psum x1 -> x0, blocking collectives: 14.7 us -> none  [body(): all_sums = lax.psum(sum_terms, 'level')]
    ppermute x0 -> x2, waiting for transfers between devices: none -> 9.03 us  [body(): all_sums = all_sums + lax.ppermute(all_sums, 'level', swap)]
    ppermute x0 -> x2, starting transfers between devices: none -> 4.78 us  [body(): all_sums = all_sums + lax.ppermute(all_sums, 'level', swap)]
  transfers between devices with their start and end apart: 4 -> 6, of which waited for: 3 -> 4; matrix products, arithmetic and copies ran while one was open for 12% -> 16% of each run, Pallas kernels for 0% -> 0%
where the time goes in v1:
time: 176 us; the launch traced here: 175 us
  waiting for transfers between devices  79.5 us (45%)
  starting transfers between devices  37.5 us (21%)
  matrix products  31.8 us (18%)
  other arithmetic  22.7 us (13%)
  local copies, waits for them, and re-layouts  2.55 us (1%)
    all_to_all x1, waiting for transfers between devices, body(): lax.all_to_all(send_rows, 'region', split_axis=0, concat_axis=0, tiled=True)  66.1 us
    another operation x2, other arithmetic  18 us
    all_to_all x1, starting transfers between devices, body(): lax.all_to_all(send_gain, 'region', split_axis=0, concat_axis=0, tiled=True)  12 us
    ppermute x2, waiting for transfers between devices, body(): all_sums = all_sums + lax.ppermute(all_sums, 'level', swap)  9.03 us
    all_to_all x1, starting transfers between devices, body(): lax.all_to_all(send_rows, 'region', split_axis=0, concat_axis=0, tiled=True)  8.95 us
    all_to_all x1, starting transfers between devices, body(): lax.all_to_all(send_innov, 'region', split_axis=0, concat_axis=0, tiled=T...  7.27 us
    dot_general x1, matrix products, body(): jnp.einsum('rso,om->rsm', placement.astype(jnp.bfloat16), obs_anomaly[0],...  6.85 us
    dot_general x1, matrix products, body(): jnp.dot(weighted.T, routed_rows, preferred_element_type=jnp.float32)  4.79 us
  transfers between devices with their start and end apart: 6, of which 4 were waited for; matrix products, arithmetic and copies ran while one was open for 16% of the time, Pallas kernels for 0%

profile of v1, /device:TPU:2, one launch (start us, length us, event | category | flops | bytes accessed | tf_op | source)
XLA Modules:
  0.0 174.9 jit_solution(8196899781956502718)
XLA Ops:
  0.0 0.8 slice_bitcast_fusion.2
  0.8 0.7 convert_element_type.111
  1.5 1.2 fusion.32
  2.9 18.0 %reduce-window.6 = s32[64,8,128]{2,1,0:T(8,128)S(1)} reduce-window(s32[64,8,128]{2,1,0:T(8,128)S(1)} %bitcast.82, s32[]{:T(128)} %constant.70.clone.1), window={size=1x1x128 pad=0_0x0_0x127_0}, to_apply=%region_0.0 | reduce-window | flops 8323072 | bytes 524292 | tf_op jit(solution)/shard_map/reduce-window
  20.9 0.1 slice.20
  21.0 0.1 copy.15
  21.2 0.1 copy.16
  21.3 0.1 add_add_fusion
  21.5 4.8 %fusion.5 = f32[64,1,96]{2,1,0:T(1,128)S(1)} fusion(s32[64,1024]{1,0:T(8,128)S(1)} %bitcast.84, pred[64,1024]{1,0:T(8,128)(4,1)S(1)} %get-tuple-element.6, bf16[1024,64,1]{0,1,2:T(8,128)(2,1)S(1)} %fusion.37), kind=kOutput, calls=%fused_computation.4 | convolution fusion | flops 25165824 | bytes 483328 | tf_op jit(solution)/shard_map/rso,or->rs/dot_general | solution.py:99
  26.2 0.6 copy.17
  26.9 12.0 %all-to-all-start = ((bf16[64,1,96]{2,1,0:T(2,128)(2,1)}), bf16[64,1,96]{2,1,0:T(2,128)(2,1)S(1)}, u32[]{:S(2)}, u32[]{:S(2)}) async-start(bf16[64,1,96]{2,1,0:T(2,128)(2,1)} %copy.17), calls=%async_computation | async-start | bytes 65536 | tf_op jit(solution)/shard_map/all_to_all | solution.py:107
  38.9 6.8 %fusion.21 = bf16[64,96,256]{2,1,0:T(8,128)(2,1)} fusion(s32[64,1024]{1,0:T(8,128)S(1)} %bitcast.85, pred[64,1024]{1,0:T(8,128)(4,1)S(1)} %get-tuple-element.6, bf16[1,1024,256]{2,1,0:T(8,128)(2,1)S(1)} %copy-done), kind=kOutput, calls=%fused_computation.23 | convolution fusion | flops 3235381248 | bytes 3997696 | tf_op jit(solution)/shard_map/rso,om->rsm/dot_general | solution.py:93
  45.8 1.7 all-to-all-done
  47.5 8.9 %all-to-all-start.1 = ((bf16[64,96,256]{2,1,0:T(8,128)(2,1)}), bf16[64,96,256]{2,1,0:T(8,128)(2,1)}, u32[]{:S(2)}, u32[]{:S(2)}) async-start(bf16[64,96,256]{2,1,0:T(8,128)(2,1)} %fusion.21), calls=%async_computation.1 | async-start | bytes 6291456 | tf_op jit(solution)/shard_map/all_to_all | solution.py:106
  56.4 0.0 copy-start.1
  56.4 4.7 %fusion.1 = f32[1,64,96]{2,0,1:T(1,128)S(1)} fusion(s32[64,1024]{1,0:T(8,128)S(1)} %bitcast.86, pred[64,1024]{1,0:T(8,128)(4,1)S(1)} %get-tuple-element.6, bf16[1,1024]{1,0:T(2,128)(2,1)S(1)} %copy-done.2), kind=kOutput, calls=%fused_computation.2 | convolution fusion | flops 25165824 | bytes 354304 | tf_op jit(solution)/shard_map/rso,o->rs/dot_general | solution.py:102
  61.1 0.6 copy.18
  61.8 0.3 convert_reduce_fusion
  62.2 66.1 %all-to-all-done.1 = bf16[64,96,256]{2,1,0:T(8,128)(2,1)} async-done(((bf16[64,96,256]{2,1,0:T(8,128)(2,1)}), bf16[64,96,256]{2,1,0:T(8,128)(2,1)}, u32[]{:S(2)}, u32[]{:S(2)}) %all-to-all-start.1) | async-done | bytes 3145760 | tf_op jit(solution)/shard_map/all_to_all | solution.py:106
  128.3 7.3 %all-to-all-start.3 = ((bf16[64,1,96]{2,1,0:T(2,128)(2,1)}), bf16[64,1,96]{2,1,0:T(2,128)(2,1)S(1)}, u32[]{:S(2)}, u32[]{:S(2)}) async-start(bf16[64,1,96]{2,1,0:T(2,128)(2,1)} %copy.18), calls=%async_computation.3 | async-start | bytes 65536 | tf_op jit(solution)/shard_map/all_to_all | solution.py:108
  135.6 4.8 %fusion.30 = f32[256,256]{1,0:T(8,128)S(1)} fusion(bf16[64,96,256]{2,1,0:T(8,128)(2,1)} %all-to-all-done.1, f32[64,96]{1,0:T(8,128)S(1)} %bitcast.89), kind=kOutput, calls=%fused_computation.34 | convolution fusion | flops 810024960 | bytes 3432448 | tf_op jit(solution)/shard_map/dot_general | solution.py:116
  140.4 1.2 broadcast_multiply_fusion
  141.5 2.7 %all-to-all-done.3 = bf16[64,1,96]{2,1,0:T(2,128)(2,1)S(1)} async-done(((bf16[64,1,96]{2,1,0:T(2,128)(2,1)}), bf16[64,1,96]{2,1,0:T(2,128)(2,1)S(1)}, u32[]{:S(2)}, u32[]{:S(2)}) %all-to-all-start.3) | async-done | bytes 12320 | tf_op jit(solution)/shard_map/all_to_all | solution.py:108
  144.2 4.5 %all-to-all-start.2 = ((f32[4,256,256]{2,1,0:T(8,128)}), f32[4,256,256]{2,1,0:T(8,128)}, u32[]{:S(2)}, u32[]{:S(2)}) async-start(f32[4,256,256]{2,1,0:T(8,128)} %broadcast_multiply_fusion), calls=%async_computation.2 | async-start | bytes 2097152 | tf_op jit(solution)/shard_map/all_to_all | solution.py:18
  148.6 2.6 %fusion.15 = f32[1,256,1]{1,0,2:T(1,128)S(1)} fusion(bf16[64,96,256]{2,1,0:T(8,128)(2,1)} %all-to-all-done.1, f32[64,96]{1,0:T(8,128)S(1)} %bitcast.90, bf16[64,1,96]{2,1,0:T(2,128)(2,1)S(1)} %all-to-all-done.3), kind=kOutput, calls=%fused_computation.17 | convolution fusion | flops 7864320 | bytes 3183616 | tf_op jit(solution)/shard_map/dot_general | solution.py:117
  151.2 0.1 broadcast_multiply_fusion.2
  151.3 2.0 %collective-permute-start = (f32[4,256]{1,0:T(4,128)S(1)}, f32[4,256]{1,0:T(4,128)S(1)}, u32[]{:S(2)}, u32[]{:S(2)}) collective-permute-start(f32[4,256]{1,0:T(4,128)S(1)} %broadcast_multiply_fusion.2), channel_id=1, source_target_pairs={{0,1},{1,0},{2,3},{3,2},{4,5},{5,4},{6,7},{7,6},{8,9},{9,8},{10,11... | collective-permute-start | bytes 12296 | tf_op jit(solution)/shard_map/ppermute | solution.py:127
  153.4 9.0 %collective-permute-done = f32[4,256]{1,0:T(4,128)S(1)} collective-permute-done((f32[4,256]{1,0:T(4,128)S(1)}, f32[4,256]{1,0:T(4,128)S(1)}, u32[]{:S(2)}, u32[]{:S(2)}) %collective-permute-start) | collective-permute-done | bytes 4128 | tf_op jit(solution)/shard_map/ppermute | solution.py:127
  162.4 0.1 fusion.78
  162.5 2.7 %collective-permute-start.1 = (f32[4,256]{1,0:T(4,128)S(1)}, f32[4,256]{1,0:T(4,128)S(1)}, u32[]{:S(2)}, u32[]{:S(2)}) collective-permute-start(f32[4,256]{1,0:T(4,128)S(1)} %fusion.78), channel_id=1, source_target_pairs={{0,2},{1,3},{2,0},{3,1},{4,6},{5,7},{6,4},{7,5},{8,10},{9,11},{10,... | collective-permute-start | bytes 12296 | tf_op jit(solution)/shard_map/ppermute | solution.py:127
  165.2 0.0 all-to-all-done.2
  165.2 1.3 reduce_sum.27
  166.5 0.7 multiply_reduce_fusion
  167.9 0.3 fusion.29
  168.3 0.4 fusion.40
  168.7 0.3 fusion.34
  169.0 0.4 fusion.28
  169.3 0.4 fusion.80
  169.7 0.4 fusion.79
  170.1 0.4 fusion.27
  170.5 0.4 fusion.81
  170.9 0.4 fusion.82
  171.3 0.4 fusion.26
  171.7 0.4 convolution_divide_fusion
  172.1 0.0 collective-permute-done.1
  172.1 0.3 convolution_bitcast_fusion
  172.3 0.3 fusion.83
  172.7 2.2 %fusion.14 = bf16[1,256,4096]{2,1,0:T(8,128)(2,1)} fusion(bf16[1,256,4096]{2,1,0:T(8,128)(2,1)S(1)} %copy-done.1, f32[4096]{0:T(1024)S(1)} %broadcast_multiply_fusion.1, f32[256,256]{1,0:T(8,128)S(1)} %convolution_divide_fusion, f32[256]{0:T(256)S(1)} %bitcast.93), kind=kOutput, calls=%fused_computation.16 | convolution fusion | flops 542310400 | bytes 4473856 | tf_op jit(solution)/shard_map/dot_general | solution.py:59
  (17 shorter events, 0.3 us)
Async XLA Ops:
  0.0 38.9 %copy-start = (bf16[1,1024,256]{2,1,0:T(8,128)(2,1)S(1)}, bf16[1,1024,256]{2,1,0:T(8,128)(2,1)}, u32[]{:S(2)}) copy-start(bf16[1,1024,256]{2,1,0:T(8,128)(2,1)} %param.7) | copy-start | bytes 1572868
  26.9 20.6 %all-to-all-start = ((bf16[64,1,96]{2,1,0:T(2,128)(2,1)}), bf16[64,1,96]{2,1,0:T(2,128)(2,1)S(1)}, u32[]{:S(2)}, u32[]{:S(2)}) async-start(bf16[64,1,96]{2,1,0:T(2,128)(2,1)} %copy.17), calls=%async_computation | async-start | bytes 65536 | tf_op jit(solution)/shard_map/all_to_all | solution.py:107
  45.8 10.7 %copy-start.2 = (bf16[1,1024]{1,0:T(2,128)(2,1)S(1)}, bf16[1,1024]{1,0:T(2,128)(2,1)}, u32[]{:S(2)}) copy-start(bf16[1,1024]{1,0:T(2,128)(2,1)} %param.8) | copy-start | bytes 6148
  47.5 80.8 %all-to-all-start.1 = ((bf16[64,96,256]{2,1,0:T(8,128)(2,1)}), bf16[64,96,256]{2,1,0:T(8,128)(2,1)}, u32[]{:S(2)}, u32[]{:S(2)}) async-start(bf16[64,96,256]{2,1,0:T(8,128)(2,1)} %fusion.21), calls=%async_computation.1 | async-start | bytes 6291456 | tf_op jit(solution)/shard_map/all_to_all | solution.py:106
  56.4 5.4 %copy-start.1 = (bf16[1,256,4096]{2,1,0:T(8,128)(2,1)S(1)}, bf16[1,256,4096]{2,1,0:T(8,128)(2,1)}, u32[]{:S(2)}) copy-start(bf16[1,256,4096]{2,1,0:T(8,128)(2,1)} %param.6) | copy-start | bytes 6291460
  128.3 15.9 %all-to-all-start.3 = ((bf16[64,1,96]{2,1,0:T(2,128)(2,1)}), bf16[64,1,96]{2,1,0:T(2,128)(2,1)S(1)}, u32[]{:S(2)}, u32[]{:S(2)}) async-start(bf16[64,1,96]{2,1,0:T(2,128)(2,1)} %copy.18), calls=%async_computation.3 | async-start | bytes 65536 | tf_op jit(solution)/shard_map/all_to_all | solution.py:108
  144.2 21.0 %all-to-all-start.2 = ((f32[4,256,256]{2,1,0:T(8,128)}), f32[4,256,256]{2,1,0:T(8,128)}, u32[]{:S(2)}, u32[]{:S(2)}) async-start(f32[4,256,256]{2,1,0:T(8,128)} %broadcast_multiply_fusion), calls=%async_computation.2 | async-start | bytes 2097152 | tf_op jit(solution)/shard_map/all_to_all | solution.py:18
  151.3 11.1 %collective-permute-start = (f32[4,256]{1,0:T(4,128)S(1)}, f32[4,256]{1,0:T(4,128)S(1)}, u32[]{:S(2)}, u32[]{:S(2)}) collective-permute-start(f32[4,256]{1,0:T(4,128)S(1)} %broadcast_multiply_fusion.2), channel_id=1, source_target_pairs={{0,1},{1,0},{2,3},{3,2},{4,5},{5,4},{6,7},{7,6},{8,9},{9,8},{10,11... | collective-permute-start | bytes 12296 | tf_op jit(solution)/shard_map/ppermute | solution.py:127
  162.5 9.6 %collective-permute-start.1 = (f32[4,256]{1,0:T(4,128)S(1)}, f32[4,256]{1,0:T(4,128)S(1)}, u32[]{:S(2)}, u32[]{:S(2)}) collective-permute-start(f32[4,256]{1,0:T(4,128)S(1)} %fusion.78), channel_id=1, source_target_pairs={{0,2},{1,3},{2,0},{3,1},{4,6},{5,7},{6,4},{7,5},{8,10},{9,11},{10,... | collective-permute-start | bytes 12296 | tf_op jit(solution)/shard_map/ppermute | solution.py:127
